TPU v7x, 256 devices: a whole 4x4x8 slice. The times are simulated.
256 devices in a mesh: grp: 4 (over y), seq: 16 (over z, core), head: 4 (over x).
Axes of the slice: x: 4, y: 4, z: 8, core: 2. Of those that a mesh axis runs over, the one named last changes fastest.
Arguments:
- keys: bfloat16 [32, 8192, 1536], P('grp', 'seq', 'head'), may hold values from -6 to 6
- values: bfloat16 [32, 8192, 1536], P('grp', 'seq', 'head'), may hold values from -6 to 6
- log_forget: float32 [32, 24, 8192], P('grp', 'head', 'seq'), may hold values from -0.6 to 0, as said below
- keep: int32 [32, 8192], P('grp', 'seq'), may hold values from 0 to 1, as said below
- merge_weight: float32 [32, 8192], P('grp', 'seq'), may hold values from 0.1 to 10
- lengths: int32 [32], P('grp'), may hold values from 64 to 8192, as said below
- route: int32 [32], P('grp'), may hold values from 0 to 31, as said below
- fresh: bfloat16 [3, 32, 1536], P(None, 'grp', 'head'), may hold values from -7.5 to 7.5
- new_forget: bfloat16 [32, 24], P('grp', 'head'), may hold values from -1 to -0.049804688
- out_weight: bfloat16 [1536, 1536], P('head', 'seq'), may hold values from -0.15625 to 0.15625
Outputs:
- compact_keys: bfloat16 [32, 4096, 1536], P('grp', 'seq', 'head')
- compact_values: bfloat16 [32, 4096, 1536], P('grp', 'seq', 'head')
- compact_decay: float32 [32, 24, 4096], P('grp', 'head', 'seq')
- layer_out: bfloat16 [32, 1536], P('grp', 'seq')
Inputs may be any that keep to these rules, and one draw needn't show every extreme that they name: `keep`: within every aligned block of 64 positions of a request, between 16 and 31 entries are 1, and some block has exactly 31. `lengths`: multiples of 64; the first request of every 8 in order has 8192. `route`: A permutation of the requests. `log_forget`: Negative.
All inputs are finite; a program needn't handle non-finite values.
Results may differ from a plain program's by a relative error of at most 0.0085.
Values may be sent and summed in bfloat16 or wider, within the bound.
A program may use at most 64 MiB of HBM per device.

v0:
```python
import jax
import jax.numpy as jnp
from jax import lax
from jax.sharding import PartitionSpec as P

BLOCK = 64
SLOTS = 32
EMPTY_LOG = -10000.0


def carried_in(value, axis, join, neutral):
    count, mine = (lax.axis_size(axis), lax.axis_index(axis))
    pieces = lax.all_gather(value, axis)
    pieces = pieces[::-1]
    mine = count - 1 - mine
    so_far = jnp.full_like(value, 0) + jnp.asarray(neutral, value.dtype)

    def turn(position, so_far):
        longer = join(so_far, pieces[position])
        return jnp.where(position < mine, longer, so_far)

    return lax.fori_loop(0, count - 1, turn, so_far)


def merged(value, axis, join):
    pieces = jax.tree.map(lambda part: lax.all_gather(part, axis), value)
    head = jax.tree.map(lambda part: part[0], pieces)
    tail = jax.tree.map(lambda part: part[1:], pieces)
    so_far, _ = lax.scan(lambda so_far, section: (join(so_far, section), None), head, tail)
    return so_far


def add_totals(earlier, later):
    return earlier + later


def merge_parts(first, second):
    top_one, sum_one, acc_one = first
    top_two, sum_two, acc_two = second
    joint = jnp.maximum(top_one, top_two)
    scale_one = jnp.exp(top_one - joint)
    scale_two = jnp.exp(top_two - joint)
    return (
        joint,
        sum_one * scale_one + sum_two * scale_two,
        acc_one * scale_one[..., None] + acc_two * scale_two[..., None],
    )


def shards(
    keys, values, log_forget, keep, merge_weight, lengths, route, fresh, new_forget, out_weight
):
    req_dev, pos_dev, width_dev = keys.shape
    heads_dev = log_forget.shape[1]
    head_size = width_dev // heads_dev
    blocks_dev = pos_dev // BLOCK
    rows_dev = blocks_dev * SLOTS
    shard = lax.axis_index("seq")
    position = shard * pos_dev + jnp.arange(pos_dev, dtype=jnp.int32)
    live = position[None, :] < lengths[:, None]
    forget = jnp.where(live[:, None, :], log_forget, 0.0)
    own_total = jnp.sum(forget, axis=2)
    inner = own_total[:, :, None] - jnp.cumsum(forget, axis=2)
    later_sum = carried_in(own_total, "seq", add_totals, jnp.zeros_like(own_total))
    log_decay = inner + later_sum[:, :, None]
    flags = keep.reshape(req_dev, blocks_dev, BLOCK)
    rank = jnp.cumsum(flags, axis=2) - 1
    slot_ids = jnp.arange(SLOTS - 1, dtype=jnp.int32)
    block_start = shard * pos_dev + jnp.arange(blocks_dev, dtype=jnp.int32) * BLOCK
    block_live = (block_start[None, :] < lengths[:, None]).astype(jnp.float32)
    chosen = (
        (flags[:, :, None, :] == 1) & (rank[:, :, None, :] == slot_ids[None, None, :, None])
    ).astype(jnp.float32)
    chosen = chosen * block_live[:, :, None, None]
    dropped = flags == 0
    weighted = jnp.where(dropped, merge_weight.reshape(req_dev, blocks_dev, BLOCK), 0.0)
    share = (
        (weighted / jnp.sum(weighted, axis=2, keepdims=True))
        .astype(jnp.bfloat16)
        .astype(jnp.float32)
    )
    merged_row = (share * block_live[:, :, None])[:, :, None, :]
    select = jnp.concatenate([chosen, merged_row], axis=2).astype(jnp.bfloat16)
    key_blocks = keys.reshape(req_dev, blocks_dev, BLOCK, width_dev)
    value_blocks = values.reshape(req_dev, blocks_dev, BLOCK, width_dev)
    packed_keys = (
        jnp.einsum("rbej,rbjc->rbec", select, key_blocks, preferred_element_type=jnp.float32)
        .astype(jnp.bfloat16)
        .reshape(req_dev, rows_dev, width_dev)
    )
    packed_values = (
        jnp.einsum("rbej,rbjc->rbec", select, value_blocks, preferred_element_type=jnp.float32)
        .astype(jnp.bfloat16)
        .reshape(req_dev, rows_dev, width_dev)
    )
    decay_blocks = log_decay.reshape(req_dev, heads_dev, blocks_dev, BLOCK)
    kept_log = jnp.einsum("rbej,rhbj->rhbe", chosen, decay_blocks, precision=lax.Precision.HIGHEST)
    filled = jnp.sum(chosen, axis=3)
    kept_log = kept_log + (1.0 - filled)[:, None, :, :] * EMPTY_LOG
    drop_mask = dropped[:, None, :, :]
    drop_peak = jnp.max(jnp.where(drop_mask, decay_blocks, -jnp.inf), axis=3)
    spread = jnp.where(drop_mask, jnp.exp(decay_blocks - drop_peak[..., None]), 0.0)
    merged_log = drop_peak + jnp.log(jnp.sum(share[:, None, :, :] * spread, axis=3))
    merged_log = jnp.where(block_live[:, None, :] > 0, merged_log, EMPTY_LOG)
    slot_log = jnp.concatenate([kept_log, merged_log[..., None]], axis=3).reshape(
        req_dev, heads_dev, rows_dev
    )
    compact_decay = jnp.exp(slot_log)
    dealt_keys, dealt_values = (
        lax.all_to_all(packed_keys, "seq", split_axis=1, concat_axis=1, tiled=True),
        lax.all_to_all(packed_values, "seq", split_axis=1, concat_axis=1, tiled=True),
    )
    arrived, arrived_forget = (
        lax.all_gather(fresh, "grp", axis=1, tiled=True),
        lax.all_gather(new_forget, "grp", axis=0, tiled=True),
    )
    picked = jnp.take(arrived, route, axis=1)
    new_log = jnp.take(arrived_forget, route, axis=0).astype(jnp.float32)
    query = picked[0].reshape(req_dev, heads_dev, head_size)
    own_key = picked[1].reshape(req_dev, heads_dev, head_size)
    own_value = picked[2].reshape(req_dev, heads_dev, head_size).astype(jnp.float32)
    scale = head_size ** (-0.5)
    key_rows = packed_keys.reshape(req_dev, rows_dev, heads_dev, head_size)
    value_rows = packed_values.reshape(req_dev, rows_dev, heads_dev, head_size)
    scores = (
        jnp.einsum("rhd,rnhd->rhn", query, key_rows, preferred_element_type=jnp.float32) * scale
        + slot_log
    )
    local_top = jnp.max(scores, axis=2)
    weights = jnp.exp(scores - local_top[..., None]).astype(jnp.bfloat16)
    local_sum = jnp.sum(weights.astype(jnp.float32), axis=2)
    local_acc = jnp.einsum("rhn,rnhd->rhd", weights, value_rows, preferred_element_type=jnp.float32)
    top, total_sum, total_acc = merged((local_top, local_sum, local_acc), "seq", merge_parts)
    own_score = jnp.sum(query.astype(jnp.float32) * own_key.astype(jnp.float32), axis=2) * scale
    cache_top = top + new_log
    joint = jnp.maximum(cache_top, own_score)
    cache_scale = jnp.exp(cache_top - joint)
    self_weight = jnp.exp(own_score - joint)
    attended = (cache_scale[..., None] * total_acc + self_weight[..., None] * own_value) / (
        cache_scale * total_sum + self_weight
    )[..., None]
    attended = attended.reshape(req_dev, width_dev).astype(jnp.bfloat16)
    partial_out = jnp.dot(attended, out_weight, preferred_element_type=jnp.float32)
    layer_out = lax.psum(partial_out, "head").astype(jnp.bfloat16)
    return (dealt_keys, dealt_values, compact_decay, layer_out)


def solution(mesh):
    return jax.shard_map(
        shards,
        mesh=mesh,
        in_specs=(
            P("grp", "seq", "head"),
            P("grp", "seq", "head"),
            P("grp", "head", "seq"),
            P("grp", "seq"),
            P("grp", "seq"),
            P("grp"),
            P("grp"),
            P(None, "grp", "head"),
            P("grp", "head"),
            P("head", "seq"),
        ),
        out_specs=(
            P("grp", "seq", "head"),
            P("grp", "seq", "head"),
            P("grp", "head", "seq"),
            P("grp", "seq"),
        ),
        check_vma=False,
    )
```

profile of v0, /device:TPU:8, one launch (start us, length us, event | category | flops | bytes accessed | tf_op | source)
XLA Modules:
  0.0 211.8 jit_solution(9465967890961578611)
XLA Ops:
  0.6 0.9 broadcast_in_dim_reshape.3
  1.6 0.8 reshape.266
  2.4 0.7 compare_select_fusion
  3.3 1.8 reduce_window_sum.24
  5.1 1.3 broadcast_compare_fusion.3
  6.9 0.6 copy-done.2
  7.5 0.7 convolution_convert_fusion
  8.2 1.1 copy-done.1
  9.4 2.1 copy.80
  11.4 8.6 %all-to-all-start.1 = ((bf16[8,256,384]{2,0,1:T(8,128)(2,1)}), bf16[8,256,384]{2,0,1:T(8,128)(2,1)}, u32[]{:S(2)}, u32[]{:S(2)}) async-start(bf16[8,256,384]{2,0,1:T(8,128)(2,1)} %copy.80), calls=%async_computation.1 | async-start | bytes 3145728 | tf_op jit(solution)/shard_map/all_to_all | solution.py:111
  20.2 0.7 select_bitcast_fusion
  20.9 6.8 %reduce-window.6 = f32[8,6,4,128]{3,0,1,2:T(8,128)S(1)} reduce-window(f32[8,6,4,128]{3,0,1,2:T(8,128)S(1)} %copy.82, f32[]{:T(128)} %constant.91.clone.1), window={size=1x1x1x128 pad=0_0x0_0x0_0x127_0}, to_apply=%region_3.4 | reduce-window | flops 3121152 | bytes 196612 | tf_op jit(solution)/shard_map/reduce-window
  27.8 1.8 select_reduce_fusion
  29.6 5.9 %reshape_reshape.7 = bf16[8,256,6,64]{3,2,1,0:T(8,128)(2,1)} reshape(bf16[8,8,32,384]{3,2,1,0:T(8,128)(2,1)} %copy-done.1) | data formatting | bytes 3145728 | tf_op jit(solution)/shard_map/reshape;reshape | solution.py:124
  35.5 32.9 %all-gather = f32[128,6]{1,0:T(8,128)S(1)} all-gather(f32[8,6]{1,0:T(8,128)S(1)} %copy.81), channel_id=2, replica_groups=mesh['grp'=4,'seq'=16,'head'=4] {'seq'}, dimensions={0}, use_global_device_ids=true | all-gather | bytes 3264 | tf_op jit(solution)/shard_map/all_gather | solution.py:13
  68.7 1.5 while.29
  70.7 0.8 fusion.25
  71.6 1.0 select_reduce_fusion.1
  73.3 0.5 copy.91
  73.7 0.8 subtract_multiply_fusion
  74.5 2.8 %fusion.13 = f32[8,6,8,31]{3,1,2,0:T(8,128)S(1)} fusion(f32[8,8]{1,0:T(8,128)S(1)} %get-tuple-element.223, s32[8,8,64]{2,1,0:T(8,128)} %copy-done.8, pred[8,8,64]{2,1,0:T(8,128)(4,1)} %copy-done.14, f32[8,6,8,64]{3,2,1,0:T(8,128)} %copy-done.5, f32[8,8,31]{2,1,0:T(8,128)S(1)} %subtract_multiply_fusion), kind=kOutput, calls=%fused_computation.25 | convolution fusion | flops 9535104 | bytes 174592 | tf_op jit(solution)/shard_map/rbej,rhbj->rhbe/dot_general | solution.py:97
  77.3 0.8 broadcast_select_fusion
  78.5 3.9 %convolution_convert_fusion.1 = bf16[8,8,32,384]{3,2,1,0:T(8,128)(2,1)} fusion(bf16[8,8,64,384]{3,2,1,0:T(8,128)(2,1)} %bitcast.75, bf16[8,8,1,64]{3,2,1,0:T(2,128)(2,1)S(1)} %copy-done.7, bf16[8,8,31,64]{3,2,1,0:T(8,128)(2,1)} %copy-done.2), kind=kOutput, calls=%fused_computation.23 | convolution fusion | flops 101974016 | bytes 4980736 | tf_op jit(solution)/shard_map/rbej,rbjc->rbec/dot_general | solution.py:87
  82.3 5.9 %reshape_reshape.6 = bf16[8,256,6,64]{3,2,1,0:T(8,128)(2,1)} reshape(bf16[8,8,32,384]{3,2,1,0:T(8,128)(2,1)} %convolution_convert_fusion.1) | data formatting | bytes 3145728 | tf_op jit(solution)/shard_map/reshape;reshape | solution.py:123
  88.3 12.2 %all_gather.32 = bf16[3,32,384]{2,1,0:T(8,128)(2,1)S(1)} all-gather(bf16[3,8,384]{2,1,0:T(8,128)(2,1)S(1)} %copy-done.18), channel_id=1, replica_groups=mesh['grp'=4,'seq'=16,'head'=4] {'grp'}, dimensions={1}, use_global_device_ids=true | all-gather | bytes 92160 | tf_op jit(solution)/shard_map/all_gather | solution.py:114
  100.6 0.6 gather_fusion
  101.3 0.6 copy-done.12
  101.9 0.6 copy-done.15
  102.6 3.1 %fusion.6 = f32[8,6,1,256]{3,2,1,0:T(1,128)S(1)} fusion(bf16[8,6,64,1]{2,3,1,0:T(2,128)(2,1)S(1)} %reshape.314, bf16[8,256,6,64]{3,2,1,0:T(8,128)(2,1)} %reshape_reshape.6), kind=kOutput, calls=%fused_computation.16 | convolution fusion | flops 1572864 | bytes 1628160 | tf_op jit(solution)/shard_map/rhd,rnhd->rhn/dot_general | solution.py:126
  105.9 0.7 convert_reduce_fusion
  106.6 2.7 %fusion.4 = f32[8,6,1,64]{3,2,1,0:T(1,128)S(1)} fusion(bf16[8,256,6,64]{3,2,1,0:T(8,128)(2,1)} %reshape_reshape.7, bf16[8,6,256,1]{2,0,1,3:T(8,128)(2,1)S(1)} %bitcast.80), kind=kOutput, calls=%fused_computation.14 | convolution fusion | flops 1572864 | bytes 1609728 | tf_op jit(solution)/shard_map/rhn,rnhd->rhd/dot_general | solution.py:132
  109.3 15.6 %all-gather.3 = f32[128,6,64]{2,0,1:T(8,128)S(1)} all-gather(f32[8,6,64]{2,0,1:T(8,128)S(1)} %bitcast.78), channel_id=5, replica_groups=mesh['grp'=4,'seq'=16,'head'=4] {'seq'}, dimensions={0}, use_global_device_ids=true | all-gather | bytes 208896 | tf_op jit(solution)/shard_map/all_gather | solution.py:26
  124.9 0.7 copy-done.3
  125.7 17.0 %all-gather.2 = f32[128,6]{1,0:T(8,128)S(1)} all-gather(f32[8,6]{1,0:T(8,128)S(1)} %copy.95), channel_id=4, replica_groups=mesh['grp'=4,'seq'=16,'head'=4] {'seq'}, dimensions={0}, use_global_device_ids=true | all-gather | bytes 3264 | tf_op jit(solution)/shard_map/all_gather | solution.py:26
  142.7 14.8 %all-gather.1 = f32[128,6]{1,0:T(8,128)S(1)} all-gather(f32[8,6]{1,0:T(8,128)S(1)} %copy.94), channel_id=3, replica_groups=mesh['grp'=4,'seq'=16,'head'=4] {'seq'}, dimensions={0}, use_global_device_ids=true | all-gather | bytes 3264 | tf_op jit(solution)/shard_map/all_gather | solution.py:26
  157.5 3.5 %copy.79 = bf16[8,256,384]{2,0,1:T(8,128)(2,1)} copy(bf16[8,256,384]{2,1,0:T(8,128)(2,1)} %bitcast.73) | data formatting | bytes 3145728 | tf_op jit(solution)/shard_map/reshape | solution.py:89
  161.0 0.6 slice_bitcast_fusion.1
  161.6 0.6 slice_bitcast_fusion.2
  162.3 5.2 %all-to-all-start = ((bf16[8,256,384]{2,0,1:T(8,128)(2,1)}), bf16[8,256,384]{2,0,1:T(8,128)(2,1)}, u32[]{:S(2)}, u32[]{:S(2)}) async-start(bf16[8,256,384]{2,0,1:T(8,128)(2,1)} %copy.79), calls=%async_computation | async-start | bytes 3145728 | tf_op jit(solution)/shard_map/all_to_all | solution.py:110
  167.6 12.3 %while.28 = (s32[]{:T(128)}, f32[8,6]{1,0:T(8,128)S(1)}, f32[8,6]{1,0:T(8,128)S(1)}, f32[8,6,64]{2,1,0:T(8,128)S(1)}, f32[15,8,6]{2,1,0:T(8,128)}, /*index=5*/f3...) while((s32[]{:T(128)}, f32[8,6]{1,0:T(8,128)S(1)}, f32[8,6]{1,0:T(8,128)S(1)}, ...), condition=%wide.region_13.14_spmd, body=%wide.region_12.13_spmd.sunk | while | flops 9506 | bytes 63453 | solution.py:29
  167.6 0.7 fusion.46
  168.4 0.7 fusion.46
  169.2 0.7 fusion.46
  170.0 0.7 fusion.46
  170.8 0.7 fusion.46
  171.7 0.7 fusion.46
  172.5 0.7 fusion.46
  173.3 0.7 fusion.46
  174.1 0.7 fusion.46
  175.0 0.7 fusion.46
  175.8 0.7 fusion.46
  176.6 0.7 fusion.46
  177.4 0.7 fusion.46
  178.2 0.7 fusion.46
  179.0 0.7 fusion.46
  179.9 0.8 reshape_squeeze.2
  180.7 0.9 fusion.29
  181.6 10.8 %all_gather.39 = bf16[32,6]{1,0:T(8,128)(2,1)S(1)} all-gather(bf16[8,6]{1,0:T(8,128)(2,1)} %param.22), channel_id=1, replica_groups=mesh['grp'=4,'seq'=16,'head'=4] {'grp'}, dimensions={0}, use_global_device_ids=true | all-gather | bytes 480 | tf_op jit(solution)/shard_map/all_gather | solution.py:115
  192.5 0.7 gather_fusion.1
  193.3 0.7 multiply_add_fusion
  194.2 1.0 fusion.38
  195.3 11.1 %psum.7 = bf16[8,96]{1,0:T(8,128)(2,1)} all-reduce(f32[8,96]{1,0:T(8,128)S(1)} %fusion.38), channel_id=1, replica_groups=mesh['grp'=4,'seq'=16,'head'=4] {'head'}, use_global_device_ids=true, to_apply=%region_15.16 | all-reduce | flops 768 | bytes 4608 | tf_op jit(solution)/shard_map/psum | solution.py:144
  206.3 2.8 %copy.103 = bf16[8,256,384]{2,1,0:T(8,128)(2,1)} copy(bf16[8,256,384]{2,0,1:T(8,128)(2,1)} %all-to-all-done.1) | data formatting | bytes 3145728
  209.1 2.8 %copy.102 = bf16[8,256,384]{2,1,0:T(8,128)(2,1)} copy(bf16[8,256,384]{2,0,1:T(8,128)(2,1)} %all-to-all-done) | data formatting | bytes 3145728
  (170 shorter events, 6.5 us)
Async XLA Ops:
  0.6 6.3 %copy-start = (bf16[8,512,384]{2,1,0:T(8,128)(2,1)S(1)}, bf16[8,512,384]{2,1,0:T(8,128)(2,1)}, u32[]{:S(2)}) copy-start(bf16[8,512,384]{2,1,0:T(8,128)(2,1)} %param.15) | copy-start | bytes 9437188
  2.4 5.8 %copy-start.9 = (f32[8,8,64]{2,1,0:T(8,128)}, f32[8,8,64]{2,1,0:T(8,128)S(1)}, u32[]{:S(2)}) copy-start(f32[8,8,64]{2,1,0:T(8,128)S(1)} %reshape.266) | copy-start | bytes 49156
  3.2 5.0 %copy-start.14 = (pred[8,8,64]{2,1,0:T(8,128)(4,1)}, pred[8,8,64]{2,1,0:T(8,128)(4,1)S(1)}, u32[]{:S(2)}) copy-start(pred[8,8,64]{2,1,0:T(8,128)(4,1)S(1)} %broadcast_compare_fusion.1) | copy-start | bytes 12292
  3.2 4.9 %copy-start.16 = (f32[8,8]{1,0:T(8,128)}, f32[8,8]{1,0:T(8,128)S(1)}, u32[]{:S(2)}) copy-start(f32[8,8]{1,0:T(8,128)S(1)} %get-tuple-element.217) | copy-start | bytes 772
  5.0 6.4 %copy-start.8 = (s32[8,8,64]{2,1,0:T(8,128)}, s32[8,8,64]{2,1,0:T(8,128)S(1)}, u32[]{:S(2)}) copy-start(s32[8,8,64]{2,1,0:T(8,128)S(1)} %broadcast_add_fusion) | copy-start | bytes 49156
  6.7 0.8 copy-start.2
  6.9 1.3 copy-start.6
  8.2 1.1 copy-start.1
  9.4 10.7 %copy-start.22 = (s32[8]{0:T(128)S(1)}, s32[8]{0:T(128)}, u32[]{:S(2)}) copy-start(s32[8]{0:T(128)} %param.19) | copy-start | bytes 100
  9.4 10.8 %copy-start.13 = (f32[8,6,512]{2,0,1:T(8,128)S(1)}, f32[8,6,512]{2,0,1:T(8,128)}, u32[]{:S(2)}) copy-start(f32[8,6,512]{2,0,1:T(8,128)} %param.16) | copy-start | bytes 294916
  11.4 150.9 %all-to-all-start.1 = ((bf16[8,256,384]{2,0,1:T(8,128)(2,1)}), bf16[8,256,384]{2,0,1:T(8,128)(2,1)}, u32[]{:S(2)}, u32[]{:S(2)}) async-start(bf16[8,256,384]{2,0,1:T(8,128)(2,1)} %copy.80), calls=%async_computation.1 | async-start | bytes 3145728 | tf_op jit(solution)/shard_map/all_to_all | solution.py:111
  27.6 7.8 %copy-start.19 = (f32[8,6]{0,1:T(8,128)S(1)}, f32[8,6]{0,1:T(8,128)}, u32[]{:S(2)}) copy-start(f32[8,6]{0,1:T(8,128)} %get-tuple-element.220) | copy-start | bytes 580
  35.5 32.9 %copy-start.17 = (f32[8,6]{1,0:T(8,128)}, f32[8,6]{1,0:T(8,128)S(1)}, u32[]{:S(2)}) copy-start(f32[8,6]{1,0:T(8,128)S(1)} %copy.81) | copy-start | bytes 580
  70.3 8.1 %copy-start.7 = (bf16[8,8,1,64]{3,2,1,0:T(2,128)(2,1)S(1)}, bf16[8,8,1,64]{3,2,1,0:T(2,128)(2,1)}, u32[]{:S(2)}) copy-start(bf16[8,8,1,64]{3,2,1,0:T(2,128)(2,1)} %copy-done.6) | copy-start | bytes 24580
  72.6 0.7 copy-start.5
  82.3 5.9 %copy-start.18 = (bf16[3,8,384]{2,1,0:T(8,128)(2,1)S(1)}, bf16[3,8,384]{2,1,0:T(8,128)(2,1)}, u32[]{:S(2)}) copy-start(bf16[3,8,384]{2,1,0:T(8,128)(2,1)} %param.21) | copy-start | bytes 55300
  82.3 18.2 %copy-start.23 = (s32[8]{0:T(128)S(1)}, s32[8]{0:T(128)}, u32[]{:S(2)}) copy-start(s32[8]{0:T(128)} %param.20) | copy-start | bytes 100
  100.6 8.7 %copy-start.20 = (s32[1024]{0:T(1024)}, s32[1024]{0:T(1024)S(1)}, u32[]{:S(2)}) copy-start(s32[1024]{0:T(1024)S(1)} %pad_clamp_fusion) | copy-start | bytes 12292
  101.2 8.1 %copy-start.21 = (pred[8]{0:T(512)(128)(4,1)}, pred[8]{0:T(512)(128)(4,1)S(1)}, u32[]{:S(2)}) copy-start(pred[8]{0:T(512)(128)(4,1)S(1)} %compare_and_fusion) | copy-start | bytes 28
  101.3 0.6 copy-start.12
  101.9 0.6 copy-start.15
  124.9 0.7 copy-start.3
  125.7 36.5 %copy-start.4 = (f32[128,6,64]{2,0,1:T(8,128)S(1)}, f32[128,6,64]{2,0,1:T(8,128)}, u32[]{:S(2)}) copy-start(f32[128,6,64]{2,0,1:T(8,128)} %copy-done.3) | copy-start | bytes 589828
  142.7 18.9 %copy-start.10 = (f32[128,6]{1,0:T(8,128)}, f32[128,6]{1,0:T(8,128)S(1)}, u32[]{:S(2)}) copy-start(f32[128,6]{1,0:T(8,128)S(1)} %all-gather.2) | copy-start | bytes 9220
  157.5 4.7 %copy-start.11 = (f32[128,6]{1,0:T(8,128)}, f32[128,6]{1,0:T(8,128)S(1)}, u32[]{:S(2)}) copy-start(f32[128,6]{1,0:T(8,128)S(1)} %all-gather.1) | copy-start | bytes 9220
  162.2 5.3 %slice-start = ((f32[128,6]{1,0:T(8,128)}), f32[8,6]{1,0:T(8,128)S(1)}, s32[]{:S(2)}) async-start(f32[128,6]{1,0:T(8,128)} %copy-done.10), calls=%async_computation.2 | async-start | bytes 8192 | tf_op jit(solution)/shard_map/slice | solution.py:27
  162.3 5.3 %slice-start.1 = ((f32[128,6]{1,0:T(8,128)}), f32[8,6]{1,0:T(8,128)S(1)}, s32[]{:S(2)}) async-start(f32[128,6]{1,0:T(8,128)} %copy-done.11), calls=%async_computation.3 | async-start | bytes 8192 | tf_op jit(solution)/shard_map/slice | solution.py:27
  162.3 46.8 %all-to-all-start = ((bf16[8,256,384]{2,0,1:T(8,128)(2,1)}), bf16[8,256,384]{2,0,1:T(8,128)(2,1)}, u32[]{:S(2)}, u32[]{:S(2)}) async-start(bf16[8,256,384]{2,0,1:T(8,128)(2,1)} %copy.79), calls=%async_computation | async-start | bytes 3145728 | tf_op jit(solution)/shard_map/all_to_all | solution.py:110
where the time goes:
time: 214 us; the launch traced here: 212 us
  blocking collectives  114 us (53%)
  local copies, waits for them, and re-layouts  35.5 us (17%)
  other arithmetic  32.4 us (15%)
  matrix products  14.2 us (7%)
  starting transfers between devices  13.8 us (6%)
    all_gather x3, blocking collectives, merged(): pieces = jax.tree.map(lambda part: lax.all_gather(part, axis), value)  47.3 us
    all_gather x1, blocking collectives, carried_in(): pieces = lax.all_gather(value, axis)  32.9 us
    all_gather x1, blocking collectives, shards(): lax.all_gather(fresh, 'grp', axis=1, tiled=True)  12.2 us
    psum x1, blocking collectives, shards(): layer_out = lax.psum(partial_out, 'head').astype(jnp.bfloat16)  11.1 us
    all_gather x1, blocking collectives, shards(): lax.all_gather(new_forget, 'grp', axis=0, tiled=True)  10.8 us
    add x15, other arithmetic, merge_parts(): sum_one * scale_one + sum_two * scale_two  10.6 us
    unnamed x50, local copies, waits for them, and re-layouts  9.61 us
    all_to_all x1, starting transfers between devices, shards(): lax.all_to_all(packed_values, 'seq', split_axis=1, concat_axis=1, tiled=T...  8.61 us
  transfers between devices with their start and end apart: 2, of which 0 were waited for; matrix products, arithmetic and copies ran while one was open for 31% of the time, Pallas kernels for 0%

commit v1 on v0

--- a/solution.py
+++ b/solution.py
@@ -108,7 +108,12 @@
     compact_decay = jnp.exp(slot_log)
     dealt_keys, dealt_values = (
         lax.all_to_all(packed_keys, "seq", split_axis=1, concat_axis=1, tiled=True),
-        lax.all_to_all(packed_values, "seq", split_axis=1, concat_axis=1, tiled=True),
+        jnp.concatenate(
+            lax.all_to_all(
+                jnp.stack(jnp.split(packed_values, lax.axis_size("seq"), axis=1)), "seq", 0, 0
+            ),
+            axis=1,
+        ),
     )
     arrived, arrived_forget = (
         lax.all_gather(fresh, "grp", axis=1, tiled=True),

time: 214 us -> 219 us (1.023)
  local copies, waits for them, and re-layouts: 35.5 us -> 42.3 us
    unnamed x50 -> x70, local copies, waits for them, and re-layouts: 9.61 us -> 15.1 us
  transfers between devices with their start and end apart: 2 -> 2, of which waited for: 0 -> 0; matrix products, arithmetic and copies ran while one was open for 31% -> 30% of each run, Pallas kernels for 0% -> 0%
where the time goes in v1:
time: 219 us; the launch traced here: 218 us
  blocking collectives  114 us (52%)
  local copies, waits for them, and re-layouts  42.3 us (19%)
  other arithmetic  31.7 us (14%)
  matrix products  14.2 us (6%)
  starting transfers between devices  14 us (6%)
    all_gather x3, blocking collectives, merged(): pieces = jax.tree.map(lambda part: lax.all_gather(part, axis), value)  47 us
    all_gather x1, blocking collectives, carried_in(): pieces = lax.all_gather(value, axis)  32.9 us
    unnamed x70, local copies, waits for them, and re-layouts  15.1 us
    all_gather x1, blocking collectives, shards(): lax.all_gather(fresh, 'grp', axis=1, tiled=True)  12.2 us
    psum x1, blocking collectives, shards(): layer_out = lax.psum(partial_out, 'head').astype(jnp.bfloat16)  11.1 us
    all_gather x1, blocking collectives, shards(): lax.all_gather(new_forget, 'grp', axis=0, tiled=True)  10.8 us
    add x15, other arithmetic, merge_parts(): sum_one * scale_one + sum_two * scale_two  10.6 us
    all_to_all x1, starting transfers between devices, shards(): lax.all_to_all(jnp.stack(jnp.split(packed_values, lax.axis_size('seq'), a...  8.75 us
  transfers between devices with their start and end apart: 2, of which 0 were waited for; matrix products, arithmetic and copies ran while one was open for 30% of the time, Pallas kernels for 0%

profile of v1, /device:TPU:8, one launch (start us, length us, event | category | flops | bytes accessed | tf_op | source)
XLA Modules:
  0.0 217.8 jit_solution(7801411780749923550)
XLA Ops:
  0.6 0.9 broadcast_in_dim_reshape.3
  1.6 0.8 reshape.272
  2.4 0.7 compare_select_fusion
  3.3 1.8 reduce_window_sum.24
  5.1 1.3 broadcast_compare_fusion.3
  6.9 0.7 convolution_convert_fusion
  7.7 0.7 fusion.38
  8.4 0.7 fusion.37
  9.1 0.7 fusion.36
  10.4 0.7 fusion.34
  11.0 0.7 fusion.33
  11.7 0.7 fusion.32
  12.3 0.7 fusion.31
  13.6 0.7 fusion.29
  14.9 0.7 fusion.27
  16.9 0.7 fusion.24
  18.2 8.7 %all-to-all-start.1 = ((bf16[16,8,16,384]{3,2,1,0:T(8,128)(2,1)}), bf16[16,8,16,384]{3,2,1,0:T(8,128)(2,1)}, u32[]{:S(2)}, u32[]{:S(2)}) async-start(bf16[16,8,16,384]{3,2,1,0:T(8,128)(2,1)} %fusion.23), calls=%async_computation.1 | async-start | bytes 3145728 | tf_op jit(solution)/shard_map/all_to_all | solution.py:112
  27.1 0.7 select_bitcast_fusion
  27.8 6.8 %reduce-window.6 = f32[8,6,4,128]{3,0,1,2:T(8,128)S(1)} reduce-window(f32[8,6,4,128]{3,0,1,2:T(8,128)S(1)} %copy.83, f32[]{:T(128)} %constant.91.clone.1), window={size=1x1x1x128 pad=0_0x0_0x0_0x127_0}, to_apply=%region_3.4 | reduce-window | flops 3121152 | bytes 196612 | tf_op jit(solution)/shard_map/reduce-window
  34.6 1.8 select_reduce_fusion
  36.5 5.9 %reshape_reshape.7 = bf16[8,256,6,64]{3,2,1,0:T(8,128)(2,1)} reshape(bf16[8,8,32,384]{3,2,1,0:T(8,128)(2,1)} %copy-done.1) | data formatting | bytes 3145728 | tf_op jit(solution)/shard_map/reshape;reshape | solution.py:129
  42.4 32.9 %all-gather = f32[128,6]{1,0:T(8,128)S(1)} all-gather(f32[8,6]{1,0:T(8,128)S(1)} %copy.82), channel_id=2, replica_groups=mesh['grp'=4,'seq'=16,'head'=4] {'seq'}, dimensions={0}, use_global_device_ids=true | all-gather | bytes 3264 | tf_op jit(solution)/shard_map/all_gather | solution.py:13
  75.6 1.5 while.29
  77.6 0.8 fusion.41
  78.5 1.0 select_reduce_fusion.1
  80.6 0.8 subtract_multiply_fusion
  81.4 2.8 %fusion.13 = f32[8,6,8,31]{3,1,2,0:T(8,128)S(1)} fusion(f32[8,8]{1,0:T(8,128)S(1)} %get-tuple-element.223, s32[8,8,64]{2,1,0:T(8,128)S(1)} %copy-done.9, pred[8,8,64]{2,1,0:T(8,128)(4,1)S(1)} %copy-done.16, f32[8,6,8,64]{3,2,1,0:T(8,128)} %copy-done.5, f32[8,8,31]{2,1,0:T(8,128)S(1)} %subtract_multiply_fusion), kind=kOutput, calls=%fused_computation.25 | convolution fusion | flops 9535104 | bytes 174592 | tf_op jit(solution)/shard_map/rbej,rhbj->rhbe/dot_general | solution.py:97
  84.7 3.9 %convolution_convert_fusion.1 = bf16[8,8,32,384]{3,2,1,0:T(8,128)(2,1)} fusion(bf16[8,8,64,384]{3,2,1,0:T(8,128)(2,1)} %bitcast.156, bf16[8,8,1,64]{3,2,1,0:T(2,128)(2,1)S(1)} %copy-done.7, bf16[8,8,31,64]{3,2,1,0:T(8,128)(2,1)} %copy-done.2), kind=kOutput, calls=%fused_computation.23 | convolution fusion | flops 101974016 | bytes 4980736 | tf_op jit(solution)/shard_map/rbej,rbjc->rbec/dot_general | solution.py:87
  88.6 5.9 %reshape_reshape.6 = bf16[8,256,6,64]{3,2,1,0:T(8,128)(2,1)} reshape(bf16[8,8,32,384]{3,2,1,0:T(8,128)(2,1)} %convolution_convert_fusion.1) | data formatting | bytes 3145728 | tf_op jit(solution)/shard_map/reshape;reshape | solution.py:128
  94.5 12.2 %all_gather.32 = bf16[3,32,384]{2,1,0:T(8,128)(2,1)S(1)} all-gather(bf16[3,8,384]{2,1,0:T(8,128)(2,1)S(1)} %copy-done.20), channel_id=1, replica_groups=mesh['grp'=4,'seq'=16,'head'=4] {'grp'}, dimensions={1}, use_global_device_ids=true | all-gather | bytes 92160 | tf_op jit(solution)/shard_map/all_gather | solution.py:119
  108.9 3.1 %fusion.6 = f32[8,6,1,256]{3,2,1,0:T(1,128)S(1)} fusion(bf16[8,6,64,1]{2,3,1,0:T(2,128)(2,1)S(1)} %reshape.322, bf16[8,256,6,64]{3,2,1,0:T(8,128)(2,1)} %reshape_reshape.6), kind=kOutput, calls=%fused_computation.16 | convolution fusion | flops 1572864 | bytes 1628160 | tf_op jit(solution)/shard_map/rhd,rnhd->rhn/dot_general | solution.py:131
  112.2 0.7 convert_reduce_fusion
  112.9 2.7 %fusion.4 = f32[8,6,1,64]{3,2,1,0:T(1,128)S(1)} fusion(bf16[8,256,6,64]{3,2,1,0:T(8,128)(2,1)} %reshape_reshape.7, bf16[8,6,256,1]{2,0,1,3:T(8,128)(2,1)S(1)} %bitcast.162), kind=kOutput, calls=%fused_computation.14 | convolution fusion | flops 1572864 | bytes 1609728 | tf_op jit(solution)/shard_map/rhn,rnhd->rhd/dot_general | solution.py:137
  115.6 15.6 %all-gather.3 = f32[128,6,64]{2,0,1:T(8,128)S(1)} all-gather(f32[8,6,64]{2,0,1:T(8,128)S(1)} %bitcast.160), channel_id=5, replica_groups=mesh['grp'=4,'seq'=16,'head'=4] {'seq'}, dimensions={0}, use_global_device_ids=true | all-gather | bytes 208896 | tf_op jit(solution)/shard_map/all_gather | solution.py:26
  131.2 0.7 copy-done.3
  132.0 16.8 %all-gather.2 = f32[128,6]{1,0:T(8,128)S(1)} all-gather(f32[8,6]{1,0:T(8,128)S(1)} %copy.96), channel_id=4, replica_groups=mesh['grp'=4,'seq'=16,'head'=4] {'seq'}, dimensions={0}, use_global_device_ids=true | all-gather | bytes 3264 | tf_op jit(solution)/shard_map/all_gather | solution.py:26
  148.8 14.6 %all-gather.1 = f32[128,6]{1,0:T(8,128)S(1)} all-gather(f32[8,6]{1,0:T(8,128)S(1)} %copy.95), channel_id=3, replica_groups=mesh['grp'=4,'seq'=16,'head'=4] {'seq'}, dimensions={0}, use_global_device_ids=true | all-gather | bytes 3264 | tf_op jit(solution)/shard_map/all_gather | solution.py:26
  163.4 3.5 %copy.80 = bf16[8,256,384]{2,0,1:T(8,128)(2,1)} copy(bf16[8,256,384]{2,1,0:T(8,128)(2,1)} %bitcast.139) | data formatting | bytes 3145728 | tf_op jit(solution)/shard_map/reshape | solution.py:89
  168.3 5.2 %all-to-all-start = ((bf16[8,256,384]{2,0,1:T(8,128)(2,1)}), bf16[8,256,384]{2,0,1:T(8,128)(2,1)}, u32[]{:S(2)}, u32[]{:S(2)}) async-start(bf16[8,256,384]{2,0,1:T(8,128)(2,1)} %copy.80), calls=%async_computation | async-start | bytes 3145728 | tf_op jit(solution)/shard_map/all_to_all | solution.py:110
  173.5 12.3 %while.28 = (s32[]{:T(128)}, f32[8,6]{1,0:T(8,128)S(1)}, f32[8,6]{1,0:T(8,128)S(1)}, f32[8,6,64]{2,1,0:T(8,128)S(1)}, f32[15,8,6]{2,1,0:T(8,128)}, /*index=5*/f3...) while((s32[]{:T(128)}, f32[8,6]{1,0:T(8,128)S(1)}, f32[8,6]{1,0:T(8,128)S(1)}, ...), condition=%wide.region_13.14_spmd, body=%wide.region_12.13_spmd.sunk | while | flops 9506 | bytes 63453 | solution.py:29
  173.6 0.7 fusion.62
  174.4 0.7 fusion.62
  175.2 0.7 fusion.62
  176.0 0.7 fusion.62
  176.9 0.7 fusion.62
  177.7 0.7 fusion.62
  178.5 0.7 fusion.62
  179.3 0.7 fusion.62
  180.1 0.7 fusion.62
  180.9 0.7 fusion.62
  181.8 0.7 fusion.62
  182.6 0.7 fusion.62
  183.4 0.7 fusion.62
  184.2 0.7 fusion.62
  185.0 0.7 fusion.62
  185.8 0.8 reshape_squeeze.2
  186.6 0.9 fusion.45
  187.6 10.8 %all_gather.39 = bf16[32,6]{1,0:T(8,128)(2,1)S(1)} all-gather(bf16[8,6]{1,0:T(8,128)(2,1)} %param.22), channel_id=1, replica_groups=mesh['grp'=4,'seq'=16,'head'=4] {'grp'}, dimensions={0}, use_global_device_ids=true | all-gather | bytes 480 | tf_op jit(solution)/shard_map/all_gather | solution.py:120
  198.4 0.7 gather_fusion.1
  199.3 0.7 multiply_add_fusion
  200.2 1.0 fusion.54
  201.2 11.1 %psum.7 = bf16[8,96]{1,0:T(8,128)(2,1)} all-reduce(f32[8,96]{1,0:T(8,128)S(1)} %fusion.54), channel_id=1, replica_groups=mesh['grp'=4,'seq'=16,'head'=4] {'head'}, use_global_device_ids=true, to_apply=%region_15.16 | all-reduce | flops 768 | bytes 4608 | tf_op jit(solution)/shard_map/psum | solution.py:149
  212.3 2.7 %copy.81 = bf16[8,16,16,384]{3,2,1,0:T(8,128)(2,1)} copy(bf16[8,16,16,384]{3,2,0,1:T(8,128)(2,1)} %bitcast.23) | data formatting | bytes 3145728 | tf_op jit(solution)/shard_map/reshape | solution.py:111
  215.0 2.8 %copy.103 = bf16[8,256,384]{2,1,0:T(8,128)(2,1)} copy(bf16[8,256,384]{2,0,1:T(8,128)(2,1)} %all-to-all-done) | data formatting | bytes 3145728
  (191 shorter events, 14.0 us)
Async XLA Ops:
  0.6 6.3 %copy-start = (bf16[8,512,384]{2,1,0:T(8,128)(2,1)S(1)}, bf16[8,512,384]{2,1,0:T(8,128)(2,1)}, u32[]{:S(2)}) copy-start(bf16[8,512,384]{2,1,0:T(8,128)(2,1)} %param.15) | copy-start | bytes 9437188
  2.4 5.2 %copy-start.10 = (f32[8,8,64]{2,1,0:T(8,128)}, f32[8,8,64]{2,1,0:T(8,128)S(1)}, u32[]{:S(2)}) copy-start(f32[8,8,64]{2,1,0:T(8,128)S(1)} %reshape.272) | copy-start | bytes 49156
  3.2 4.5 %copy-start.15 = (pred[8,8,64]{2,1,0:T(8,128)(4,1)}, pred[8,8,64]{2,1,0:T(8,128)(4,1)S(1)}, u32[]{:S(2)}) copy-start(pred[8,8,64]{2,1,0:T(8,128)(4,1)S(1)} %broadcast_compare_fusion.1) | copy-start | bytes 12292
  3.2 4.4 %copy-start.18 = (f32[8,8]{1,0:T(8,128)}, f32[8,8]{1,0:T(8,128)S(1)}, u32[]{:S(2)}) copy-start(f32[8,8]{1,0:T(8,128)S(1)} %get-tuple-element.217) | copy-start | bytes 772
  5.0 2.6 %copy-start.8 = (s32[8,8,64]{2,1,0:T(8,128)}, s32[8,8,64]{2,1,0:T(8,128)S(1)}, u32[]{:S(2)}) copy-start(s32[8,8,64]{2,1,0:T(8,128)S(1)} %broadcast_add_fusion) | copy-start | bytes 49156
  6.7 1.0 copy-start.2
  6.9 0.8 copy-start.6
  7.7 9.9 %copy-start.1 = (bf16[8,8,32,384]{3,2,1,0:T(8,128)(2,1)}, bf16[8,8,32,384]{3,2,1,0:T(8,128)(2,1)S(1)}, u32[]{:S(2)}) copy-start(bf16[8,8,32,384]{3,2,1,0:T(8,128)(2,1)S(1)} %convolution_convert_fusion) | copy-start | bytes 4718596
  18.2 8.8 %copy-start.25 = (s32[8]{0:T(128)S(1)}, s32[8]{0:T(128)}, u32[]{:S(2)}) copy-start(s32[8]{0:T(128)} %param.19) | copy-start | bytes 100
  18.2 8.9 %copy-start.14 = (f32[8,6,512]{2,0,1:T(8,128)S(1)}, f32[8,6,512]{2,0,1:T(8,128)}, u32[]{:S(2)}) copy-start(f32[8,6,512]{2,0,1:T(8,128)} %param.16) | copy-start | bytes 294916
  18.2 150.1 %all-to-all-start.1 = ((bf16[16,8,16,384]{3,2,1,0:T(8,128)(2,1)}), bf16[16,8,16,384]{3,2,1,0:T(8,128)(2,1)}, u32[]{:S(2)}, u32[]{:S(2)}) async-start(bf16[16,8,16,384]{3,2,1,0:T(8,128)(2,1)} %fusion.23), calls=%async_computation.1 | async-start | bytes 3145728 | tf_op jit(solution)/shard_map/all_to_all | solution.py:112
  36.5 5.9 %copy-start.21 = (f32[8,6]{0,1:T(8,128)S(1)}, f32[8,6]{0,1:T(8,128)}, u32[]{:S(2)}) copy-start(f32[8,6]{0,1:T(8,128)} %get-tuple-element.220) | copy-start | bytes 580
  42.4 32.9 %copy-start.19 = (f32[8,6]{1,0:T(8,128)}, f32[8,6]{1,0:T(8,128)S(1)}, u32[]{:S(2)}) copy-start(f32[8,6]{1,0:T(8,128)S(1)} %copy.82) | copy-start | bytes 580
  77.2 4.2 %copy-start.9 = (s32[8,8,64]{2,1,0:T(8,128)S(1)}, s32[8,8,64]{2,1,0:T(8,128)}, u32[]{:S(2)}) copy-start(s32[8,8,64]{2,1,0:T(8,128)} %copy-done.8) | copy-start | bytes 49156
  77.2 4.2 %copy-start.16 = (pred[8,8,64]{2,1,0:T(8,128)(4,1)S(1)}, pred[8,8,64]{2,1,0:T(8,128)(4,1)}, u32[]{:S(2)}) copy-start(pred[8,8,64]{2,1,0:T(8,128)(4,1)} %copy-done.15) | copy-start | bytes 12292
  77.2 7.0 %copy-start.23 = (pred[8,8]{1,0:T(8,128)(4,1)S(1)}, pred[8,8]{1,0:T(8,128)(4,1)}, u32[]{:S(2)}) copy-start(pred[8,8]{1,0:T(8,128)(4,1)} %get-tuple-element.222) | copy-start | bytes 196
  79.5 0.7 copy-start.5
  81.4 3.3 %copy-start.7 = (bf16[8,8,1,64]{3,2,1,0:T(2,128)(2,1)S(1)}, bf16[8,8,1,64]{3,2,1,0:T(2,128)(2,1)}, u32[]{:S(2)}) copy-start(bf16[8,8,1,64]{3,2,1,0:T(2,128)(2,1)} %copy-done.6) | copy-start | bytes 24580
  88.6 5.9 %copy-start.20 = (bf16[3,8,384]{2,1,0:T(8,128)(2,1)S(1)}, bf16[3,8,384]{2,1,0:T(8,128)(2,1)}, u32[]{:S(2)}) copy-start(bf16[3,8,384]{2,1,0:T(8,128)(2,1)} %param.21) | copy-start | bytes 55300
  88.6 18.2 %copy-start.26 = (s32[8]{0:T(128)S(1)}, s32[8]{0:T(128)}, u32[]{:S(2)}) copy-start(s32[8]{0:T(128)} %param.20) | copy-start | bytes 100
  106.8 5.1 %copy-start.22 = (s32[1024]{0:T(1024)}, s32[1024]{0:T(1024)S(1)}, u32[]{:S(2)}) copy-start(s32[1024]{0:T(1024)S(1)} %pad_clamp_fusion) | copy-start | bytes 12292
  107.4 4.5 %copy-start.24 = (pred[8]{0:T(512)(128)(4,1)}, pred[8]{0:T(512)(128)(4,1)S(1)}, u32[]{:S(2)}) copy-start(pred[8]{0:T(512)(128)(4,1)S(1)} %compare_and_fusion) | copy-start | bytes 28
  107.5 0.6 copy-start.13
  108.2 0.6 copy-start.17
  131.2 0.7 copy-start.3
  148.8 18.1 %copy-start.11 = (f32[128,6]{1,0:T(8,128)}, f32[128,6]{1,0:T(8,128)S(1)}, u32[]{:S(2)}) copy-start(f32[128,6]{1,0:T(8,128)S(1)} %all-gather.2) | copy-start | bytes 9220
  163.4 4.2 %copy-start.12 = (f32[128,6]{1,0:T(8,128)}, f32[128,6]{1,0:T(8,128)S(1)}, u32[]{:S(2)}) copy-start(f32[128,6]{1,0:T(8,128)S(1)} %all-gather.1) | copy-start | bytes 9220
  163.4 4.8 %copy-start.4 = (f32[128,6,64]{2,0,1:T(8,128)S(1)}, f32[128,6,64]{2,0,1:T(8,128)}, u32[]{:S(2)}) copy-start(f32[128,6,64]{2,0,1:T(8,128)} %copy-done.3) | copy-start | bytes 589828
  168.3 5.3 %slice-start = ((f32[128,6]{1,0:T(8,128)}), f32[8,6]{1,0:T(8,128)S(1)}, s32[]{:S(2)}) async-start(f32[128,6]{1,0:T(8,128)} %copy-done.11), calls=%async_computation.2 | async-start | bytes 8192 | tf_op jit(solution)/shard_map/slice | solution.py:27
  168.3 5.3 %slice-start.1 = ((f32[128,6]{1,0:T(8,128)}), f32[8,6]{1,0:T(8,128)S(1)}, s32[]{:S(2)}) async-start(f32[128,6]{1,0:T(8,128)} %copy-done.12), calls=%async_computation.3 | async-start | bytes 8192 | tf_op jit(solution)/shard_map/slice | solution.py:27
  168.3 46.7 %all-to-all-start = ((bf16[8,256,384]{2,0,1:T(8,128)(2,1)}), bf16[8,256,384]{2,0,1:T(8,128)(2,1)}, u32[]{:S(2)}, u32[]{:S(2)}) async-start(bf16[8,256,384]{2,0,1:T(8,128)(2,1)} %copy.80), calls=%async_computation | async-start | bytes 3145728 | tf_op jit(solution)/shard_map/all_to_all | solution.py:110
